TPU v7x, 256 devices: a whole 4x4x8 slice. The times are simulated.
256 devices in a mesh: freq: 64 (over y, z, core), sky: 4 (over x).
Axes of the slice: x: 4, y: 4, z: 8, core: 2. Of those that a mesh axis runs over, the one named last changes fastest.
Arguments:
- sky_maps: bfloat16 [1024, 96, 4096], P('freq', 'sky'), may hold values from -240 to 240
- beam_index: int32 [1024], P('freq'), may hold values from 0 to 7
- beam_taps: float32 [8, 31], replicated, may hold values from 0.05 to 1
- start_seed: int32 [1024, 16], replicated, may hold values from -64 to 64
Outputs:
- cleaned: bfloat16 [1024, 256, 1536], P(None, ('freq', 'sky'))
All inputs are finite; a program needn't handle non-finite values.
Results may differ from a plain program's by a relative error of at most 0.0079.
The roundings to bfloat16 on the way count: a program that leaves them out, or rounds other values in their place, can miss the bound.
Values may be sent and summed in bfloat16 or wider, within the bound.
No kernel may reach another device: no remote copies, remote signals or barrier semaphores. Data moves between devices by JAX's collectives and lax.ppermute only.
A program may use at most 64 MiB of HBM per device.

v0:
```python
import jax
import jax.numpy as jnp
from jax import lax
from jax.sharding import PartitionSpec as P

ITERS = 8


def with_halo(x, sides, width):
    for axis, dim in sides:
        size, length = (lax.axis_size(axis), x.shape[dim])
        up = [(i, (i + 1) % size) for i in range(size - 1)]
        down = [(j, i) for i, j in up]
        last = lax.slice_in_dim(x, length - width, length, axis=dim)
        leading = lax.slice_in_dim(x, 0, width, axis=dim)
        before = lax.ppermute(last, axis, up)
        after = lax.ppermute(leading, axis, down)
        x = jnp.concatenate([before, x, after], axis=dim)
    return x


def column_pass(padded, kernels, strip_rows, half_taps, tap_count):
    row_pass = jnp.zeros((padded.shape[0], strip_rows, padded.shape[2]), jnp.float32)
    for offset in range(tap_count):
        row_pass = row_pass + kernels[:, offset, None, None] * padded[
            :, offset : offset + strip_rows, :
        ].astype(jnp.float32)
    columns = padded.shape[2]
    widened = jnp.pad(row_pass, ((0, 0), (0, 0), (half_taps, half_taps)))
    col_pass = jnp.zeros(row_pass.shape, jnp.float32)
    for offset in range(tap_count):
        col_pass = (
            col_pass + kernels[:, offset, None, None] * widened[:, :, offset : offset + columns]
        )
    return col_pass.astype(jnp.bfloat16)


def orthonormal(images):
    gram_matrix = jnp.dot(images.T, images, precision=lax.Precision.HIGHEST)
    factor = jnp.linalg.cholesky(gram_matrix)
    return lax.linalg.triangular_solve(
        factor, images, left_side=False, lower=True, transpose_a=True
    )


def local_covariance(tile_data):
    return lax.dot_general(
        tile_data, tile_data, (((1,), (1,)), ((), ())), preferred_element_type=jnp.float32
    )


def body(sky_maps, beam_index, beam_taps, start_seed):
    channels, strip_rows, columns = sky_maps.shape
    beam_count, tap_count = beam_taps.shape
    half_taps = (tap_count - 1) // 2
    onehot = (beam_index[:, None] == jnp.arange(beam_count, dtype=jnp.int32)[None, :]).astype(
        jnp.float32
    )
    tap_rows = jnp.dot(onehot, beam_taps, precision=lax.Precision.HIGHEST)
    kernels = tap_rows / jnp.sum(tap_rows, axis=1, keepdims=True)
    padded = with_halo(sky_maps, (("sky", 1),), half_taps)
    smoothed = column_pass(padded, kernels, strip_rows, half_taps, tap_count)
    freq_count = lax.axis_size("freq")
    sky_count = lax.axis_size("sky")
    tile_cols = columns // freq_count
    grouped = lax.all_to_all(
        smoothed.reshape(channels, strip_rows, freq_count, tile_cols),
        "freq",
        split_axis=2,
        concat_axis=0,
        tiled=True,
    )
    all_chans = channels * freq_count
    tile_data = grouped.reshape(all_chans, strip_rows * tile_cols)
    wide_tile = tile_data.astype(jnp.float32)
    total_pixels = strip_rows * columns * sky_count
    subspace = start_seed.astype(jnp.float32)
    covariance = lax.psum(local_covariance(tile_data), ("freq", "sky")) / total_pixels
    for sweep in range(ITERS):
        images = jnp.dot(covariance, subspace, precision=lax.Precision.HIGHEST)
        subspace = orthonormal(images)
    coeffs = jnp.dot(subspace.T, wide_tile, precision=lax.Precision.HIGHEST)
    cleaned = (wide_tile - jnp.dot(subspace, coeffs, precision=lax.Precision.HIGHEST)).astype(
        jnp.bfloat16
    )
    return cleaned.reshape(all_chans, 1, strip_rows * tile_cols)


def solution(mesh):
    return jax.shard_map(
        body,
        mesh=mesh,
        in_specs=(P("freq", "sky", None), P("freq"), P(), P()),
        out_specs=P(None, ("freq", "sky"), None),
        check_vma=False,
    )
```

profile of v0, /device:TPU:2, one launch (start us, length us, event | category | flops | bytes accessed | tf_op | source)
XLA Modules:
  0.0 664.6 jit_solution(16235698417459183960)
XLA Ops:
  6.5 2.9 fusion.109
  10.7 3.4 collective-permute-start
  15.2 2.6 collective-permute-start.1
  19.4 37.7 %collective-permute-done = bf16[16,15,4096]{2,0,1:T(8,128)(2,1)S(1)} collective-permute-done((bf16[16,15,4096]{2,0,1:T(8,128)(2,1)S(1)}, bf16[16,15,4096]{2,0,1:T(8,128)(2,1)S(1)}, u32[]{:S(2)}, u32[]{:S(2)}) %collective-permute-start) | collective-permute-done | bytes 1966112 | tf_op jit(solution)/shard_map/ppermute | solution.py:16
  58.2 3.2 collective-permute-done.1
  62.5 40.9 %multiply_add_fusion = f32[16,24,4096]{2,1,0:T(8,128)S(1)} fusion(bf16[16,24,4096]{2,1,0:T(8,128)(2,1)S(1)} %copy-done.2, bf16[16,15,4096]{2,1,0:T(8,128)(2,1)S(1)} %copy.24, bf16[16,39,4096]{2,1,0:T(8,128)(2,1)S(1)} %copy_dynamic-update-slice_fusion, f32[16]{0:T(128)S(1)} %get-tuple-element.8, f32[16]{0:T(128)S(1)} %get-tuple-element.9, ...), kind=kLoop, calls=%fused_computation.62 | loop fusion | flops 215482368 | bytes 58591168 | tf_op jit(solution)/shard_map/add | solution.py:25
  103.4 50.4 %add_convert_fusion = bf16[16,24,4096]{2,1,0:T(8,128)(2,1)S(1)} fusion(f32[16,24,4096]{2,1,0:T(8,128)S(1)} %multiply_add_fusion, f32[16]{0:T(128)S(1)} %get-tuple-element.8, f32[16]{0:T(128)S(1)} %get-tuple-element.9, f32[16]{0:T(128)S(1)} %get-tuple-element.10, f32[16]{0:T(128)S(1)} %get-tuple-element.11, f32[16]{0:T(128)S(1)} %get-tuple-element.12, ...), kind=kLoop, calls=%fused_computation.29 | loop fusion | flops 97517568 | bytes 9439168 | tf_op jit(solution)/shard_map/convert_element_type | solution.py:35
  153.8 7.9 %reshape.54 = bf16[16,24,64,64]{3,2,1,0:T(8,128)(2,1)} reshape(bf16[16,24,4096]{2,1,0:T(8,128)(2,1)S(1)} %add_convert_fusion) | data formatting | bytes 6291456 | tf_op jit(solution)/shard_map/reshape | solution.py:67
  161.7 9.5 %copy.40 = bf16[16,24,64,64]{3,1,0,2:T(8,128)(2,1)} copy(bf16[16,24,64,64]{3,2,1,0:T(8,128)(2,1)} %reshape.54) | data formatting | bytes 6291456 | tf_op jit(solution)/shard_map/reshape | solution.py:67
  171.2 9.7 %reshape.118 = bf16[64,2,12288]{2,1,0:T(2,128)(2,1)S(1)} reshape(bf16[64,16,24,64]{3,2,1,0:T(8,128)(2,1)} %bitcast.141) | data formatting | bytes 6291456
  180.9 85.0 %all_to_all.15 = bf16[64,2,12288]{2,1,0:T(2,128)(2,1)} all-to-all(bf16[64,2,12288]{2,1,0:T(2,128)(2,1)S(1)} %reshape.118), channel_id=1, replica_groups=mesh['freq'=64,'sky'=4] {'freq'}, dimensions={0} | all-to-all | bytes 6291456 | tf_op jit(solution)/shard_map/all_to_all | solution.py:66
  265.9 11.1 %reshape.119 = bf16[64,16,24,64]{3,2,1,0:T(8,128)(2,1)} reshape(bf16[64,2,12288]{2,1,0:T(2,128)(2,1)} %all_to_all.15) | data formatting | bytes 6291456
  277.0 7.4 %bitcast_bitcast_fusion = bf16[64,16,24,1,64]{4,2,1,0,3:T(8,128)(2,1)} fusion(bf16[64,16,24,64]{3,2,1,0:T(8,128)(2,1)} %reshape.119), kind=kLoop, calls=%fused_computation.224 | loop fusion | bytes 6291456 | tf_op jit(solution)/shard_map/all_to_all | solution.py:66
  284.5 7.9 %reshape.55 = bf16[1024,1536]{1,0:T(8,128)(2,1)S(1)} reshape(bf16[64,16,24,1,64]{4,2,1,0,3:T(8,128)(2,1)} %bitcast_bitcast_fusion) | data formatting | bytes 6291456 | tf_op jit(solution)/shard_map/reshape | solution.py:74
  292.4 5.4 fusion.111
  297.8 267.5 %all-reduce.3.cloned.1.call-done = f32[1024,1024]{1,0:T(8,128)} async-done(((f32[1024,1024]{1,0:T(8,128)}), f32[1024,1024]{1,0:T(8,128)}) %all-reduce.3.cloned.1.call-update) | async-done | bytes 4194320 | tf_op jit(solution)/shard_map/psum | solution.py:78
  565.3 5.9 fusion.50
  571.5 1.5 cholesky.134
  575.8 5.9 fusion.48
  582.0 1.5 cholesky.145
  586.3 5.9 fusion.46
  596.8 5.9 fusion.44
  602.9 1.6 cholesky.167
  607.4 5.9 fusion.42
  613.6 1.5 cholesky.178
  617.9 5.9 fusion.40
  624.1 1.5 cholesky.189
  628.4 5.9 fusion.38
  634.5 1.5 cholesky.200
  638.9 5.9 fusion.36
  645.2 1.5 cholesky.211
  650.9 6.7 %fusion.21 = bf16[1024,1,1536]{2,0,1:T(8,128)(2,1)} fusion(f32[1024,16]{0,1:T(8,128)S(1)} %convolution_bitcast_fusion, f32[16,1536]{1,0:T(8,128)S(1)} %fusion.120, bf16[1024,1536]{1,0:T(8,128)(2,1)S(1)} %reshape.55), kind=kOutput, calls=%fused_computation.63 | convolution fusion | flops 306708480 | bytes 6455296 | tf_op jit(solution)/shard_map/dot_general | solution.py:83
  (87 shorter events, 33.9 us)
Async XLA Ops:
  6.5 11.3 %copy-start = (f32[8,31]{1,0:T(8,128)S(1)}, f32[8,31]{1,0:T(8,128)}, u32[]{:S(2)}) copy-start(f32[8,31]{1,0:T(8,128)} %param.9) | copy-start | bytes 2980
  6.5 11.3 %copy-start.4 = (s32[16]{0:T(128)S(1)}, s32[16]{0:T(128)}, u32[]{:S(2)}) copy-start(s32[16]{0:T(128)} %param.8) | copy-start | bytes 196
  6.5 558.8 %all-reduce.3.cloned.1.call-start = ((), (), s32[]{:S(2)}) async-start(), calls=%async_computation.1 | async-start | bytes 8388608 | tf_op jit(solution)/shard_map/psum | solution.py:78
  9.5 9.6 %copy-start.2 = (bf16[16,24,4096]{2,1,0:T(8,128)(2,1)S(1)}, bf16[16,24,4096]{2,1,0:T(8,128)(2,1)}, u32[]{:S(2)}) copy-start(bf16[16,24,4096]{2,1,0:T(8,128)(2,1)} %param.7) | copy-start | bytes 9437188
  10.7 46.5 %collective-permute-start = (bf16[16,15,4096]{2,0,1:T(8,128)(2,1)S(1)}, bf16[16,15,4096]{2,0,1:T(8,128)(2,1)S(1)}, u32[]{:S(2)}, u32[]{:S(2)}) collective-permute-start(bf16[16,15,4096]{2,0,1:T(8,128)(2,1)S(1)} %copy.36), channel_id=1, source_target_pairs={{0,1},{1,2},{2,3},{4,5},{5,6},{6,7},{8,9},{9,10},{10,11},{12,13},{... | collective-permute-start | bytes 5898248 | tf_op jit(solution)/shard_map/ppermute | solution.py:16
  15.2 46.2 %collective-permute-start.1 = (bf16[16,15,4096]{2,0,1:T(8,128)(2,1)S(1)}, bf16[16,15,4096]{2,0,1:T(8,128)(2,1)S(1)}, u32[]{:S(2)}, u32[]{:S(2)}) collective-permute-start(bf16[16,15,4096]{2,0,1:T(8,128)(2,1)S(1)} %copy.37), channel_id=1, source_target_pairs={{1,0},{2,1},{3,2},{5,4},{6,5},{7,6},{9,8},{10,9},{11,10},{13,12},{... | collective-permute-start | bytes 5898248 | tf_op jit(solution)/shard_map/ppermute | solution.py:17
  292.4 273.0 %copy-start.3 = (s32[1024,16]{0,1:T(8,128)S(1)}, s32[1024,16]{0,1:T(8,128)}, u32[]{:S(2)}) copy-start(s32[1024,16]{0,1:T(8,128)} %param.10) | copy-start | bytes 196612
  638.6 18.9 %copy-start.1 = (f32[8,31]{1,0:T(8,128)S(1)}, f32[8,31]{1,0:T(8,128)}, u32[]{:S(2)}) copy-start(f32[8,31]{1,0:T(8,128)} %param.9) | copy-start | bytes 2980
Sparse Core Ops, SparseCore 0:
  297.9 267.3 all-reduce.2
where the time goes:
time: 671 us; the launch traced here: 665 us
  waiting for transfers between devices  308 us (46%)
  other arithmetic  124 us (18%)
  blocking collectives  85 us (13%)
  matrix products  64.5 us (10%)
  local copies, waits for them, and re-layouts  62.9 us (9%)
  between operations  13.9 us (2%)
    psum x1, waiting for transfers between devices, body(): lax.psum(local_covariance(tile_data), ('freq', 'sky')) / total_pixels  268 us
    all_to_all x1, blocking collectives, body(): lax.all_to_all(smoothed.reshape(channels, strip_rows, freq_count, tile_co...  85 us
    convert_element_type x1, other arithmetic, column_pass(): return col_pass.astype(jnp.bfloat16)  50.4 us
    dot_general x8, matrix products, body(): images = jnp.dot(covariance, subspace, precision=lax.Precision.HIGHEST)  47 us
    add x1, other arithmetic, column_pass(): row_pass + kernels[:, offset, None, None] * padded[:, offset:offset + str...  40.9 us
    ppermute x1, waiting for transfers between devices, with_halo(): before = lax.ppermute(last, axis, up)  37.7 us
    unnamed x15, local copies, waits for them, and re-layouts  23.5 us
    another operation x24, other arithmetic, orthonormal(): factor = jnp.linalg.cholesky(gram_matrix)  17.5 us
  transfers between devices with their start and end apart: 3, of which 3 were waited for; matrix products, arithmetic and copies ran while one was open for 1% of the time, Pallas kernels for 0%

commit v1 on v0

--- a/solution.py
+++ b/solution.py
@@ -75,7 +75,7 @@
     wide_tile = tile_data.astype(jnp.float32)
     total_pixels = strip_rows * columns * sky_count
     subspace = start_seed.astype(jnp.float32)
-    covariance = lax.psum(local_covariance(tile_data), ("freq", "sky")) / total_pixels
+    covariance = lax.psum(lax.psum(local_covariance(tile_data), "sky"), "freq") / total_pixels
     for sweep in range(ITERS):
         images = jnp.dot(covariance, subspace, precision=lax.Precision.HIGHEST)
         subspace = orthonormal(images)

time: 671 us -> 698 us (1.040)
  waiting for transfers between devices: 308 us -> 335 us
    psum x1 -> x2, waiting for transfers between devices: 268 us -> 294 us  [the longest x1 201 us: body(): lax.psum(lax.psum(local_covariance(tile_data), 'sky'), 'freq')]
  transfers between devices with their start and end apart: 3 -> 4, of which waited for: 3 -> 4; matrix products, arithmetic and copies ran while one was open for 1% -> 1% of each run, Pallas kernels for 0% -> 0%
where the time goes in v1:
time: 698 us; the launch traced here: 692 us
  waiting for transfers between devices  335 us (48%)
  other arithmetic  124 us (18%)
  blocking collectives  85 us (12%)
  matrix products  64.1 us (9%)
  local copies, waits for them, and re-layouts  62.9 us (9%)
  between operations  13.9 us (2%)
    psum x1, waiting for transfers between devices, body(): lax.psum(lax.psum(local_covariance(tile_data), 'sky'), 'freq')  201 us
    psum x1, waiting for transfers between devices, body(): lax.psum(local_covariance(tile_data), 'sky')  93.7 us
    all_to_all x1, blocking collectives, body(): lax.all_to_all(smoothed.reshape(channels, strip_rows, freq_count, tile_co...  85 us
    convert_element_type x1, other arithmetic, column_pass(): return col_pass.astype(jnp.bfloat16)  50.4 us
    dot_general x8, matrix products, body(): images = jnp.dot(covariance, subspace, precision=lax.Precision.HIGHEST)  47.2 us
    add x1, other arithmetic, column_pass(): row_pass + kernels[:, offset, None, None] * padded[:, offset:offset + str...  40.9 us
    ppermute x1, waiting for transfers between devices, with_halo(): before = lax.ppermute(last, axis, up)  37.7 us
    unnamed x15, local copies, waits for them, and re-layouts  23.5 us
  transfers between devices with their start and end apart: 4, of which 4 were waited for; matrix products, arithmetic and copies ran while one was open for 1% of the time, Pallas kernels for 0%

profile of v1, /device:TPU:2, one launch (start us, length us, event | category | flops | bytes accessed | tf_op | source)
XLA Modules:
  0.0 691.6 jit_solution(10457013735751264317)
XLA Ops:
  6.5 2.9 fusion.109
  10.7 3.4 collective-permute-start
  15.2 2.6 collective-permute-start.1
  19.4 37.7 %collective-permute-done = bf16[16,15,4096]{2,0,1:T(8,128)(2,1)S(1)} collective-permute-done((bf16[16,15,4096]{2,0,1:T(8,128)(2,1)S(1)}, bf16[16,15,4096]{2,0,1:T(8,128)(2,1)S(1)}, u32[]{:S(2)}, u32[]{:S(2)}) %collective-permute-start) | collective-permute-done | bytes 1966112 | tf_op jit(solution)/shard_map/ppermute | solution.py:16
  58.2 3.2 collective-permute-done.1
  62.5 40.9 %multiply_add_fusion = f32[16,24,4096]{2,1,0:T(8,128)S(1)} fusion(bf16[16,24,4096]{2,1,0:T(8,128)(2,1)S(1)} %copy-done.2, bf16[16,15,4096]{2,1,0:T(8,128)(2,1)S(1)} %copy.24, bf16[16,39,4096]{2,1,0:T(8,128)(2,1)S(1)} %copy_dynamic-update-slice_fusion, f32[16]{0:T(128)S(1)} %get-tuple-element.8, f32[16]{0:T(128)S(1)} %get-tuple-element.9, ...), kind=kLoop, calls=%fused_computation.62 | loop fusion | flops 215482368 | bytes 58591168 | tf_op jit(solution)/shard_map/add | solution.py:25
  103.4 50.4 %add_convert_fusion = bf16[16,24,4096]{2,1,0:T(8,128)(2,1)S(1)} fusion(f32[16,24,4096]{2,1,0:T(8,128)S(1)} %multiply_add_fusion, f32[16]{0:T(128)S(1)} %get-tuple-element.8, f32[16]{0:T(128)S(1)} %get-tuple-element.9, f32[16]{0:T(128)S(1)} %get-tuple-element.10, f32[16]{0:T(128)S(1)} %get-tuple-element.11, f32[16]{0:T(128)S(1)} %get-tuple-element.12, ...), kind=kLoop, calls=%fused_computation.29 | loop fusion | flops 97517568 | bytes 9439168 | tf_op jit(solution)/shard_map/convert_element_type | solution.py:35
  153.8 7.9 %reshape.54 = bf16[16,24,64,64]{3,2,1,0:T(8,128)(2,1)} reshape(bf16[16,24,4096]{2,1,0:T(8,128)(2,1)S(1)} %add_convert_fusion) | data formatting | bytes 6291456 | tf_op jit(solution)/shard_map/reshape | solution.py:67
  161.7 9.5 %copy.40 = bf16[16,24,64,64]{3,1,0,2:T(8,128)(2,1)} copy(bf16[16,24,64,64]{3,2,1,0:T(8,128)(2,1)} %reshape.54) | data formatting | bytes 6291456 | tf_op jit(solution)/shard_map/reshape | solution.py:67
  171.2 9.7 %reshape.118 = bf16[64,2,12288]{2,1,0:T(2,128)(2,1)S(1)} reshape(bf16[64,16,24,64]{3,2,1,0:T(8,128)(2,1)} %bitcast.141) | data formatting | bytes 6291456
  180.9 85.0 %all_to_all.15 = bf16[64,2,12288]{2,1,0:T(2,128)(2,1)} all-to-all(bf16[64,2,12288]{2,1,0:T(2,128)(2,1)S(1)} %reshape.118), channel_id=1, replica_groups=mesh['freq'=64,'sky'=4] {'freq'}, dimensions={0} | all-to-all | bytes 6291456 | tf_op jit(solution)/shard_map/all_to_all | solution.py:66
  265.9 11.1 %reshape.119 = bf16[64,16,24,64]{3,2,1,0:T(8,128)(2,1)} reshape(bf16[64,2,12288]{2,1,0:T(2,128)(2,1)} %all_to_all.15) | data formatting | bytes 6291456
  277.0 7.4 %bitcast_bitcast_fusion = bf16[64,16,24,1,64]{4,2,1,0,3:T(8,128)(2,1)} fusion(bf16[64,16,24,64]{3,2,1,0:T(8,128)(2,1)} %reshape.119), kind=kLoop, calls=%fused_computation.224 | loop fusion | bytes 6291456 | tf_op jit(solution)/shard_map/all_to_all | solution.py:66
  284.5 7.9 %reshape.55 = bf16[1024,1536]{1,0:T(8,128)(2,1)S(1)} reshape(bf16[64,16,24,1,64]{4,2,1,0,3:T(8,128)(2,1)} %bitcast_bitcast_fusion) | data formatting | bytes 6291456 | tf_op jit(solution)/shard_map/reshape | solution.py:74
  292.4 5.0 fusion.111
  297.9 93.7 %all-reduce.4.cloned.1.call-done = f32[1024,1024]{1,0:T(8,128)} async-done(((f32[1024,1024]{1,0:T(8,128)}), f32[1024,1024]{1,0:T(8,128)}) %all-reduce.4.cloned.1.call-update) | async-done | bytes 4194320 | tf_op jit(solution)/shard_map/psum | solution.py:78
  391.6 200.7 %all-reduce.6.cloned.1.call-done = f32[1024,1024]{1,0:T(8,128)} async-done(((f32[1024,1024]{1,0:T(8,128)}), f32[1024,1024]{1,0:T(8,128)}) %all-reduce.6.cloned.1.call-update) | async-done | bytes 4194320 | tf_op jit(solution)/shard_map/psum | solution.py:78
  592.4 5.9 fusion.50
  598.5 1.5 cholesky.134
  602.8 5.9 fusion.48
  609.0 1.5 cholesky.145
  613.3 5.9 fusion.46
  619.5 1.5 cholesky.156
  623.8 5.9 fusion.44
  630.0 1.6 cholesky.167
  634.4 5.9 fusion.42
  640.6 1.5 cholesky.178
  644.9 5.9 fusion.40
  651.1 1.5 cholesky.189
  655.4 5.9 fusion.38
  665.9 6.1 fusion.36
  677.9 6.7 fusion.21
  (90 shorter events, 35.7 us)
Async XLA Ops:
  6.5 11.3 %copy-start = (f32[8,31]{1,0:T(8,128)S(1)}, f32[8,31]{1,0:T(8,128)}, u32[]{:S(2)}) copy-start(f32[8,31]{1,0:T(8,128)} %param.9) | copy-start | bytes 2980
  6.5 11.3 %copy-start.4 = (s32[16]{0:T(128)S(1)}, s32[16]{0:T(128)}, u32[]{:S(2)}) copy-start(s32[16]{0:T(128)} %param.8) | copy-start | bytes 196
  6.5 385.1 %all-reduce.4.cloned.1.call-start = ((), (), s32[]{:S(2)}) async-start(), calls=%async_computation.1 | async-start | bytes 8388608 | tf_op jit(solution)/shard_map/psum | solution.py:78
  9.5 9.6 %copy-start.2 = (bf16[16,24,4096]{2,1,0:T(8,128)(2,1)S(1)}, bf16[16,24,4096]{2,1,0:T(8,128)(2,1)}, u32[]{:S(2)}) copy-start(bf16[16,24,4096]{2,1,0:T(8,128)(2,1)} %param.7) | copy-start | bytes 9437188
  10.7 46.5 %collective-permute-start = (bf16[16,15,4096]{2,0,1:T(8,128)(2,1)S(1)}, bf16[16,15,4096]{2,0,1:T(8,128)(2,1)S(1)}, u32[]{:S(2)}, u32[]{:S(2)}) collective-permute-start(bf16[16,15,4096]{2,0,1:T(8,128)(2,1)S(1)} %copy.36), channel_id=1, source_target_pairs={{0,1},{1,2},{2,3},{4,5},{5,6},{6,7},{8,9},{9,10},{10,11},{12,13},{... | collective-permute-start | bytes 5898248 | tf_op jit(solution)/shard_map/ppermute | solution.py:16
  15.2 46.2 %collective-permute-start.1 = (bf16[16,15,4096]{2,0,1:T(8,128)(2,1)S(1)}, bf16[16,15,4096]{2,0,1:T(8,128)(2,1)S(1)}, u32[]{:S(2)}, u32[]{:S(2)}) collective-permute-start(bf16[16,15,4096]{2,0,1:T(8,128)(2,1)S(1)} %copy.37), channel_id=1, source_target_pairs={{1,0},{2,1},{3,2},{5,4},{6,5},{7,6},{9,8},{10,9},{11,10},{13,12},{... | collective-permute-start | bytes 5898248 | tf_op jit(solution)/shard_map/ppermute | solution.py:17
  297.4 294.9 %copy-start.3 = (s32[1024,16]{0,1:T(8,128)S(1)}, s32[1024,16]{0,1:T(8,128)}, u32[]{:S(2)}) copy-start(s32[1024,16]{0,1:T(8,128)} %param.10) | copy-start | bytes 196612
  297.5 294.9 %all-reduce.6.cloned.1.call-start = ((), (), s32[]{:S(2)}) async-start(), calls=%async_computation.2 | async-start | bytes 8388608 | tf_op jit(solution)/shard_map/psum | solution.py:78
  665.6 18.9 %copy-start.1 = (f32[8,31]{1,0:T(8,128)S(1)}, f32[8,31]{1,0:T(8,128)}, u32[]{:S(2)}) copy-start(f32[8,31]{1,0:T(8,128)} %param.9) | copy-start | bytes 2980
Sparse Core Ops, SparseCore 0:
  297.6 93.9 all-reduce.3
  395.1 197.1 all-reduce.5
